TPU v7x, 32 devices: a whole 2x2x4 slice. The times are simulated.
32 devices in a mesh: vocab: 4 (over z), expert: 8 (over y, x, core).
Axes of the slice: x: 2, y: 2, z: 4, core: 2. Of those that a mesh axis runs over, the one named last changes fastest.
Arguments:
- token_ids: int32 [1024], replicated, may hold values from 0 to 75967
- word_mask: int32 [75968], P('vocab'), may hold values 0 or 1
- embed_table: bfloat16 [75968, 4096], P('vocab', 'expert'), may hold values from -6 to 6
- attn_out: bfloat16 [1024, 4096], P('expert', 'vocab'), may hold values from -6 to 6
- in_gain: float32 [4096], replicated, may hold values from 0.25 to 1.75
- key_weight: bfloat16 [4096, 512], P(None, 'vocab'), may hold values from -0.09375 to 0.09375
- key_gain: float32 [128], replicated, may hold values from 0.25 to 1.75
- post_gain: float32 [4096], replicated, may hold values from 0.25 to 1.75
- routes: int32 [1024, 8], P('expert'), may hold values from 0 to 15, all different within a row; in each aligned block of 128 rows (0 to 127, 128 to 255, ...) at most 96 rows name the same one
- gate_ints: int32 [1024, 8], P('expert'), may hold values from 1 to 63
- w_gate: bfloat16 [32, 4096, 768], P(('expert', 'vocab')), may hold values from -0.09375 to 0.09375
- w_up: bfloat16 [32, 4096, 768], P(('expert', 'vocab')), may hold values from -0.09375 to 0.09375
- w_down: bfloat16 [32, 768, 4096], P(('expert', 'vocab')), may hold values from -0.15625 to 0.15625
Outputs:
- expert_out: bfloat16 [1024, 4096], P('expert', 'vocab')
- key_heads: bfloat16 [1024, 512], P('expert', 'vocab')
Inputs may be any that keep to these rules, and one draw needn't show every extreme that they name: `routes`: each row names 8 different experts; within the 128 rows of one index of expert no expert is named by more than 96 rows, and in some such blocks one is named by exactly 96.
All inputs are finite; a program needn't handle non-finite values. No bound on the sum of `word_mask` on one device may be relied on, other than what follows from the above.
Results may differ from a plain program's by a relative error of at most 0.008.
Values may be sent and summed in bfloat16 or wider, within the bound.
A program may use at most 192 MiB of HBM per device.

v0:
```python
import jax
import jax.numpy as jnp
from jax import lax
from jax.sharding import PartitionSpec as P


def rms_rows(values, scale_gain):
    inverse_rms = lax.rsqrt(jnp.mean(values * values, axis=-1, keepdims=True) + 1e-06)
    return values * inverse_rms * scale_gain


def on_device(
    token_ids,
    word_mask,
    embed_table,
    attn_out,
    in_gain,
    key_weight,
    key_gain,
    post_gain,
    routes,
    gate_ints,
    w_gate,
    w_up,
    w_down,
):
    n_vocab = lax.axis_size("vocab")
    n_expert = lax.axis_size("expert")
    vocab_rows = embed_table.shape[0]
    experts_total = n_expert * n_vocab // 2
    whole_mesh = ("expert", "vocab")
    my_vocab = lax.axis_index("vocab")
    my_expert = (lax.axis_index("expert") * n_vocab + my_vocab) // 2
    gate_share = gate_ints.astype(jnp.float32) / jnp.sum(gate_ints, axis=1, keepdims=True).astype(
        jnp.float32
    )
    onehot = routes[:, :, None] == jnp.arange(experts_total, dtype=jnp.int32)[None, None, :]
    share_of = jnp.sum(jnp.where(onehot, gate_share[:, :, None], 0.0), axis=1)
    all_shares = lax.all_gather(share_of, "expert", axis=0, tiled=True)
    my_share = lax.dynamic_slice_in_dim(all_shares, my_expert, 1, axis=1)
    attn_rows = lax.all_to_all(attn_out, "vocab", split_axis=0, concat_axis=1, tiled=True)
    local_ids = token_ids - my_vocab * vocab_rows
    inside = (local_ids >= 0) & (local_ids < vocab_rows)
    safe_ids = jnp.clip(local_ids, 0, vocab_rows - 1)
    keep_row = inside & (word_mask[safe_ids] == 1)
    partial_value = jnp.where(
        keep_row[:, None], embed_table[safe_ids], jnp.zeros_like(embed_table[:1])
    )
    moved_rows = lax.all_to_all(partial_value, "expert", split_axis=0, concat_axis=1, tiled=True)
    rows = lax.psum_scatter(moved_rows, "vocab", scatter_dimension=0, tiled=True)
    rows = rows.astype(jnp.float32)
    mid_rows = (rows + attn_rows.astype(jnp.float32)).astype(jnp.bfloat16)
    expert_in = rms_rows(mid_rows.astype(jnp.float32), post_gain).astype(jnp.bfloat16)
    tokens_in = lax.all_gather(expert_in, whole_mesh, axis=0, tiled=True)
    normed_rows = rms_rows(rows, in_gain).astype(jnp.bfloat16)
    key_rows = lax.all_gather(normed_rows, "vocab", axis=0, tiled=True)
    raw_keys = jnp.dot(key_rows, key_weight, preferred_element_type=jnp.float32)
    key_heads = rms_rows(raw_keys, key_gain).astype(jnp.bfloat16)
    gate_val = jnp.dot(tokens_in, w_gate[0], preferred_element_type=jnp.float32)
    up_val = jnp.dot(tokens_in, w_up[0], preferred_element_type=jnp.float32)
    hidden = (jax.nn.silu(gate_val) * up_val).astype(jnp.bfloat16)
    parts = jnp.dot(hidden, w_down[0], preferred_element_type=jnp.float32)
    weighted = (parts * my_share).astype(jnp.bfloat16)
    by_tokens = lax.psum_scatter(weighted, "expert", scatter_dimension=0, tiled=True)
    expert_out = lax.psum_scatter(by_tokens, "vocab", scatter_dimension=1, tiled=True)
    return (expert_out, key_heads)


def solution(mesh):
    return jax.shard_map(
        on_device,
        mesh=mesh,
        in_specs=(
            P(),
            P("vocab"),
            P("vocab", "expert"),
            P("expert", "vocab"),
            P(),
            P(None, "vocab"),
            P(),
            P(),
            P("expert", None),
            P("expert", None),
            P(("expert", "vocab"), None, None),
            P(("expert", "vocab"), None, None),
            P(("expert", "vocab"), None, None),
        ),
        out_specs=(P("expert", "vocab"), P("expert", "vocab")),
        check_vma=False,
    )
```

profile of v0, /device:TPU:0, one launch (start us, length us, event | category | flops | bytes accessed | tf_op | source)
XLA Modules:
  0.0 324.6 jit_solution(1872449881291243474)
XLA Ops:
  7.2 0.0 copy-start
  7.2 0.0 reduce-scatter.10.cloned.1.call-start
  7.2 0.8 fusion.14
  8.0 5.9 %gather_fusion = s32[1024]{0:T(1024)S(1)} fusion(s32[18992]{0:T(1024)} %param.14, s32[1024]{0:T(1024)S(1)} %fusion.14), kind=kCustom, calls=%fused_computation | custom fusion | bytes 12288 | tf_op jit(solution)/shard_map/gather | solution.py:45
  13.9 0.7 and_bitcast_fusion
  14.6 13.0 %gather_fusion.1 = bf16[1024,512]{1,0:T(8,128)(2,1)S(1)} fusion(bf16[18992,512]{1,0:T(8,128)(2,1)} %param.15, s32[1024]{0:T(1024)S(1)} %fusion.14), kind=kCustom, calls=%fused_computation.1 | custom fusion | bytes 2101248 | tf_op jit(solution)/shard_map/gather | solution.py:47
  27.7 0.0 copy-start.1
  27.7 0.0 copy-start.2
  27.7 0.0 copy-start.3
  27.7 0.7 copy.30
  28.4 0.0 copy-start.4
  28.4 0.0 copy-start.5
  28.4 0.1 broadcast_select_fusion
  28.5 20.3 %all_to_all.29 = bf16[8,128,512]{1,2,0:T(8,128)(2,1)S(1)} all-to-all(bf16[8,128,512]{1,2,0:T(8,128)(2,1)S(1)} %broadcast_select_fusion), channel_id=1, replica_groups=mesh['vocab'=4,'expert'=8] {'expert'}, dimensions={0} | all-to-all | bytes 2097152 | tf_op jit(solution)/shard_map/all_to_all | solution.py:49
  48.8 1.3 copy.34
  50.1 0.0 reduce-scatter.10.cloned.1.call-update
  50.1 0.0 all-gather.3.cloned.1.call-start
  50.2 0.0 copy-done.1
  50.2 19.2 %all_to_all.30 = bf16[4,32,1024]{2,1,0:T(8,128)(2,1)S(1)} all-to-all(bf16[4,32,1024]{2,1,0:T(8,128)(2,1)S(1)} %bitcast.33), channel_id=1, replica_groups=mesh['vocab'=4,'expert'=8] {'vocab'}, dimensions={0} | all-to-all | bytes 524288 | tf_op jit(solution)/shard_map/all_to_all | solution.py:41
  69.5 10.3 %reduce-scatter.10.cloned.1.call-done = bf16[32,4096]{1,0:T(8,128)(2,1)} async-done(((bf16[128,4096]{1,0:T(8,128)(2,1)}), bf16[32,4096]{1,0:T(8,128)(2,1)}) %reduce-scatter.10.cloned.1.call-update) | async-done | bytes 262160 | tf_op jit(solution)/shard_map/reduce_scatter | solution.py:50
  79.8 1.2 fusion.11
  81.0 0.0 copy-done.2
  81.0 0.0 copy-done.3
  81.0 1.9 fusion.13
  82.9 0.0 all-gather.3.cloned.1.call-update
  82.9 0.0 reduce-scatter.6.cloned.1.call-start
  83.0 0.0 copy-done.4
  83.1 0.0 copy-done.5
  83.1 9.1 %all_gather.10 = f32[1024,16]{0,1:T(8,128)S(1)} all-gather(f32[128,16]{0,1:T(8,128)S(1)} %select_reduce_fusion), channel_id=1, replica_groups=mesh['vocab'=4,'expert'=8] {'expert'}, dimensions={0}, use_global_device_ids=true | all-gather | bytes 73728 | tf_op jit(solution)/shard_map/all_gather | solution.py:39
  92.2 67.2 %all-gather.3.cloned.1.call-done = bf16[1024,4096]{1,0:T(8,128)(2,1)} async-done(((bf16[32,4096]{1,0:T(8,128)(2,1)}), bf16[1024,4096]{1,0:T(8,128)(2,1)}) %all-gather.3.cloned.1.call-update) | async-done | bytes 8388624 | tf_op jit(solution)/shard_map/all_gather | solution.py:54
  159.3 0.0 copy-start.7
  159.3 0.0 slice-start
  159.3 11.0 %fusion.1 = f32[1024,768]{1,0:T(8,128)S(1)} fusion(bf16[1024,4096]{1,0:T(8,128)(2,1)} %all-gather.3.cloned.1.call-done, bf16[1,4096,768]{2,1,0:T(8,128)(2,1)} %param.24), kind=kOutput, calls=%fused_computation.4 | convolution fusion | flops 6442450944 | bytes 17825792 | tf_op jit(solution)/shard_map/dot_general | solution.py:60
  170.4 0.0 copy-done.7
  170.4 0.0 slice-start.1
  170.4 9.9 %multiply_convert_fusion.1 = bf16[1024,768]{1,0:T(8,128)(2,1)S(1)} fusion(f32[1024,768]{1,0:T(8,128)S(1)} %fusion.1, bf16[1024,4096]{1,0:T(8,128)(2,1)S(1)} %copy-done.7, bf16[1,4096,768]{2,1,0:T(8,128)(2,1)} %param.23), kind=kOutput, calls=%fused_computation.8 | convolution fusion | flops 6447169536 | bytes 19398656 | tf_op jit(solution)/shard_map/dot_general | solution.py:59
  180.3 0.0 slice-done
  180.3 0.0 slice-done.1
  180.4 8.9 %multiply_convert_fusion = bf16[1024,4096]{1,0:T(8,128)(2,1)} fusion(f32[1024]{0:T(1024)S(1)} %bitcast.34, bf16[1024,768]{1,0:T(8,128)(2,1)S(1)} %multiply_convert_fusion.1, bf16[1,768,4096]{2,1,0:T(8,128)(2,1)S(1)} %bitcast.36), kind=kOutput, calls=%fused_computation.2 | convolution fusion | flops 6450839552 | bytes 16257024 | tf_op jit(solution)/shard_map/dot_general | solution.py:62
  189.2 0.0 copy-start.6
  189.2 0.0 reduce-scatter.6.cloned.1.call-update
  189.3 0.0 all-gather.5.cloned.1.call-start
  189.3 0.5 all-gather.5.cloned.1.call-update
  189.8 0.0 reduce-scatter.8.cloned.1.call-start
  189.9 69.4 %reduce-scatter.6.cloned.1.call-done = bf16[128,4096]{1,0:T(8,128)(2,1)} async-done(((bf16[1024,4096]{1,0:T(8,128)(2,1)}), bf16[128,4096]{1,0:T(8,128)(2,1)}) %reduce-scatter.6.cloned.1.call-update) | async-done | bytes 1048592 | tf_op jit(solution)/shard_map/reduce_scatter | solution.py:64
  259.3 0.0 reduce-scatter.8.cloned.1.call-update
  259.3 29.4 %all-gather.5.cloned.1.call-done = bf16[128,4096]{1,0:T(8,128)(2,1)} async-done(((bf16[32,4096]{1,0:T(8,128)(2,1)}), bf16[128,4096]{1,0:T(8,128)(2,1)}) %all-gather.5.cloned.1.call-update) | async-done | bytes 1048592 | tf_op jit(solution)/shard_map/all_gather | solution.py:56
  288.7 0.0 copy-done
  288.7 1.8 multiply_reduce_fusion
  290.5 0.0 copy-done.6
  290.5 0.1 multiply_convert_fusion.2
  290.6 0.7 copy.33
  291.3 26.8 %reduce-scatter.8.cloned.1.call-done = bf16[128,1024]{1,0:T(8,128)(2,1)} async-done(((bf16[128,4096]{1,0:T(8,128)(2,1)}), bf16[128,1024]{1,0:T(8,128)(2,1)}) %reduce-scatter.8.cloned.1.call-update) | async-done | bytes 262160 | tf_op jit(solution)/shard_map/reduce_scatter | solution.py:65
  (10 shorter events, 0.2 us)
Async XLA Ops:
  7.2 281.5 %copy-start = (bf16[4096,128]{1,0:T(8,128)(2,1)S(1)}, bf16[4096,128]{1,0:T(8,128)(2,1)}, u32[]{:S(2)}) copy-start(bf16[4096,128]{1,0:T(8,128)(2,1)} %param.18) | copy-start | bytes 3145732
  7.2 72.6 %reduce-scatter.10.cloned.1.call-start = ((), (), s32[]{:S(2)}) async-start(), calls=%async_computation.9 | async-start | bytes 1310720 | tf_op jit(solution)/shard_map/reduce_scatter | solution.py:50
  27.7 22.5 %copy-start.1 = (bf16[128,1024]{1,0:T(8,128)(2,1)S(1)}, bf16[128,1024]{1,0:T(8,128)(2,1)}, u32[]{:S(2)}) copy-start(bf16[128,1024]{1,0:T(8,128)(2,1)} %param.16) | copy-start | bytes 786436
  27.7 53.3 %copy-start.2 = (f32[4096]{0:T(1024)S(1)}, f32[4096]{0:T(1024)}, u32[]{:S(2)}) copy-start(f32[4096]{0:T(1024)} %param.17) | copy-start | bytes 49156
  27.7 53.3 %copy-start.3 = (f32[4096]{0:T(1024)S(1)}, f32[4096]{0:T(1024)}, u32[]{:S(2)}) copy-start(f32[4096]{0:T(1024)} %param.20) | copy-start | bytes 49156
  28.4 54.6 %copy-start.4 = (s32[128,8]{0,1:T(8,128)S(1)}, s32[128,8]{0,1:T(8,128)}, u32[]{:S(2)}) copy-start(s32[128,8]{0,1:T(8,128)} %param.22) | copy-start | bytes 12292
  28.4 54.7 %copy-start.5 = (s32[128,8]{0,1:T(8,128)S(1)}, s32[128,8]{0,1:T(8,128)}, u32[]{:S(2)}) copy-start(s32[128,8]{0,1:T(8,128)} %param.21) | copy-start | bytes 12292
  50.1 109.2 %all-gather.3.cloned.1.call-start = ((), (), s32[]{:S(2)}) async-start(), calls=%async_computation.5 | async-start | bytes 8650752 | tf_op jit(solution)/shard_map/all_gather | solution.py:54
  82.9 176.4 %reduce-scatter.6.cloned.1.call-start = ((), (), s32[]{:S(2)}) async-start(), calls=%async_computation.6 | async-start | bytes 9437184 | tf_op jit(solution)/shard_map/reduce_scatter | solution.py:64
  159.3 11.1 %copy-start.7 = (bf16[1024,4096]{1,0:T(8,128)(2,1)S(1)}, bf16[1024,4096]{1,0:T(8,128)(2,1)}, u32[]{:S(2)}) copy-start(bf16[1024,4096]{1,0:T(8,128)(2,1)} %all-gather.3.cloned.1.call-done) | copy-start | bytes 25165828
  159.3 21.0 %slice-start = ((s8[6291456]{0:T(1024)(128)(4,1)}), s8[4194304]{0:T(1024)(128)(4,1)S(1)}, s32[]{:S(2)}) async-start(s8[6291456]{0:T(1024)(128)(4,1)} %bitcast.35), calls=%async_computation.10 | async-start | bytes 8388608
  170.4 10.0 %slice-start.1 = ((s8[6291456]{0:T(1024)(128)(4,1)}), s8[2097152]{0:T(1024)(128)(4,1)S(1)}, s32[]{:S(2)}) async-start(s8[6291456]{0:T(1024)(128)(4,1)} %bitcast.35), calls=%async_computation.11 | async-start | bytes 4194304
  189.2 101.2 %copy-start.6 = (f32[128]{0:T(128)S(1)}, f32[128]{0:T(128)}, u32[]{:S(2)}) copy-start(f32[128]{0:T(128)} %param.19) | copy-start | bytes 1540
  189.3 99.4 %all-gather.5.cloned.1.call-start = ((), (), s32[]{:S(2)}) async-start(), calls=%async_computation.8 | async-start | bytes 1310720 | tf_op jit(solution)/shard_map/all_gather | solution.py:56
  189.8 128.2 %reduce-scatter.8.cloned.1.call-start = ((), (), s32[]{:S(2)}) async-start(), calls=%async_computation.7 | async-start | bytes 1310720 | tf_op jit(solution)/shard_map/reduce_scatter | solution.py:65
Sparse Core Ops, SparseCore 0:
  50.2 29.4 reduce-scatter.9
  83.7 75.5 all-gather.2
  189.4 69.8 reduce-scatter.5
  260.7 27.9 all-gather.4
  291.4 26.6 reduce-scatter.7
where the time goes:
time: 325 us
  waiting for transfers between devices  204 us (63%)
  blocking collectives  48.6 us (15%)
  matrix products  31.6 us (10%)
  local copies, waits for them, and re-layouts  21.7 us (7%)
  between operations  14 us (4%)
  other arithmetic  4.83 us (1%)
    reduce_scatter x1, waiting for transfers between devices, on_device(): lax.psum_scatter(weighted, 'expert', scatter_dimension=0, tiled=True)  69.4 us
    all_gather x1, waiting for transfers between devices, on_device(): tokens_in = lax.all_gather(expert_in, whole_mesh, axis=0, tiled=True)  67.2 us
    all_gather x1, waiting for transfers between devices, on_device(): key_rows = lax.all_gather(normed_rows, 'vocab', axis=0, tiled=True)  29.4 us
    reduce_scatter x1, waiting for transfers between devices, on_device(): lax.psum_scatter(by_tokens, 'vocab', scatter_dimension=1, tiled=True)  26.8 us
    all_to_all x1, blocking collectives, on_device(): lax.all_to_all(partial_value, 'expert', split_axis=0, concat_axis=1, tile...  20.3 us
    all_to_all x1, blocking collectives, on_device(): lax.all_to_all(attn_out, 'vocab', split_axis=0, concat_axis=1, tiled=True)  19.2 us
    gather x2, local copies, waits for them, and re-layouts, on_device(): embed_table[safe_ids]  13.7 us
    dot_general x1, matrix products, on_device(): up_val = jnp.dot(tokens_in, w_up[0], preferred_element_type=jnp.float32)  11 us
  transfers between devices with their start and end apart: 5, of which 5 were waited for; matrix products, arithmetic and copies ran while one was open for 1% of the time, Pallas kernels for 0%

commit v1 on v0

--- a/solution.py
+++ b/solution.py
@@ -2,6 +2,27 @@
 import jax.numpy as jnp
 from jax import lax
 from jax.sharding import PartitionSpec as P
+
+
+def ring_gather(x, axis, dim):
+    size, here, width = (lax.axis_size(axis), lax.axis_index(axis), x.shape[dim])
+    ahead = [(i, (i + 1) % size) for i in range(size)]
+    left = [(i, (i - 1) % size) for i in range(size)]
+    result = jnp.zeros((*x.shape[:dim], size * width, *x.shape[dim + 1 :]), x.dtype)
+    result = lax.dynamic_update_slice_in_dim(result, x, here * width, axis=dim)
+    from_left = from_right = x
+    halfway = size // 2
+    for hop in range(1, halfway + 1):
+        from_left = lax.ppermute(from_left, axis, ahead)
+        result = lax.dynamic_update_slice_in_dim(
+            result, from_left, (here - hop) % size * width, axis=dim
+        )
+        if hop < size - halfway:
+            from_right = lax.ppermute(from_right, axis, left)
+            result = lax.dynamic_update_slice_in_dim(
+                result, from_right, (here + hop) % size * width, axis=dim
+            )
+    return result
 
 
 def rms_rows(values, scale_gain):
@@ -53,7 +74,7 @@
     expert_in = rms_rows(mid_rows.astype(jnp.float32), post_gain).astype(jnp.bfloat16)
     tokens_in = lax.all_gather(expert_in, whole_mesh, axis=0, tiled=True)
     normed_rows = rms_rows(rows, in_gain).astype(jnp.bfloat16)
-    key_rows = lax.all_gather(normed_rows, "vocab", axis=0, tiled=True)
+    key_rows = ring_gather(normed_rows, "vocab", 0)
     raw_keys = jnp.dot(key_rows, key_weight, preferred_element_type=jnp.float32)
     key_heads = rms_rows(raw_keys, key_gain).astype(jnp.bfloat16)
     gate_val = jnp.dot(tokens_in, w_gate[0], preferred_element_type=jnp.float32)

time: 325 us -> 300 us (0.923)
  waiting for transfers between devices: 204 us -> 174 us
  starting transfers between devices: 0.2 us -> 5.09 us
    all_gather x1 -> x0, waiting for transfers between devices: 29.4 us -> none  [on_device(): key_rows = lax.all_gather(normed_rows, 'vocab', axis=0, tiled=True)]
    ppermute x0 -> x3, waiting for transfers between devices: none -> 18.3 us  [the longest x2 10.1 us: ring_gather(): from_left = lax.ppermute(from_left, axis, ahead)]
    reduce_scatter x1, waiting for transfers between devices: 26.8 us -> 10.1 us  [on_device(): lax.psum_scatter(by_tokens, 'vocab', scatter_dimension=1, tiled=True)]
    ppermute x0 -> x3, starting transfers between devices: none -> 4.93 us  [the longest x1 3.37 us: ring_gather(): from_right = lax.ppermute(from_right, axis, left)]
  transfers between devices with their start and end apart: 5 -> 7, of which waited for: 5 -> 6; matrix products, arithmetic and copies ran while one was open for 1% -> 1% of each run, Pallas kernels for 0% -> 0%
where the time goes in v1:
time: 300 us; the launch traced here: 299 us
  waiting for transfers between devices  174 us (58%)
  blocking collectives  48.6 us (16%)
  matrix products  30.4 us (10%)
  local copies, waits for them, and re-layouts  22.6 us (8%)
  between operations  14.1 us (5%)
  starting transfers between devices  5.09 us (2%)
  other arithmetic  4.81 us (2%)
    reduce_scatter x1, waiting for transfers between devices, on_device(): lax.psum_scatter(weighted, 'expert', scatter_dimension=0, tiled=True)  67.4 us
    all_gather x1, waiting for transfers between devices, on_device(): tokens_in = lax.all_gather(expert_in, whole_mesh, axis=0, tiled=True)  67.3 us
    all_to_all x1, blocking collectives, on_device(): lax.all_to_all(partial_value, 'expert', split_axis=0, concat_axis=1, tile...  20.3 us
    all_to_all x1, blocking collectives, on_device(): lax.all_to_all(attn_out, 'vocab', split_axis=0, concat_axis=1, tiled=True)  19.2 us
    gather x2, local copies, waits for them, and re-layouts, on_device(): embed_table[safe_ids]  13.7 us
    dot_general x1, matrix products, on_device(): up_val = jnp.dot(tokens_in, w_up[0], preferred_element_type=jnp.float32)  11 us
    reduce_scatter x1, waiting for transfers between devices, on_device(): lax.psum_scatter(moved_rows, 'vocab', scatter_dimension=0, tiled=True)  10.3 us
    reduce_scatter x1, waiting for transfers between devices, on_device(): lax.psum_scatter(by_tokens, 'vocab', scatter_dimension=1, tiled=True)  10.1 us
  transfers between devices with their start and end apart: 7, of which 6 were waited for; matrix products, arithmetic and copies ran while one was open for 1% of the time, Pallas kernels for 0%

profile of v1, /device:TPU:0, one launch (start us, length us, event | category | flops | bytes accessed | tf_op | source)
XLA Modules:
  0.0 299.2 jit_solution(8097365811429780878)
XLA Ops:
  7.2 0.0 copy-start
  7.2 0.0 reduce-scatter.10.cloned.1.call-start
  7.2 0.8 fusion.14
  8.0 5.9 %gather_fusion = s32[1024]{0:T(1024)S(1)} fusion(s32[18992]{0:T(1024)} %param.14, s32[1024]{0:T(1024)S(1)} %fusion.14), kind=kCustom, calls=%fused_computation | custom fusion | bytes 12288 | tf_op jit(solution)/shard_map/gather | solution.py:66
  13.9 0.7 and_bitcast_fusion
  14.6 13.0 %gather_fusion.1 = bf16[1024,512]{1,0:T(8,128)(2,1)S(1)} fusion(bf16[18992,512]{1,0:T(8,128)(2,1)} %param.15, s32[1024]{0:T(1024)S(1)} %fusion.14), kind=kCustom, calls=%fused_computation.1 | custom fusion | bytes 2101248 | tf_op jit(solution)/shard_map/gather | solution.py:68
  27.7 0.0 copy-start.2
  27.7 0.0 copy-start.3
  27.7 0.7 copy.30
  28.3 0.0 copy-start.5
  28.4 0.0 copy-start.6
  28.4 0.1 broadcast_select_fusion
  28.5 20.3 %all_to_all.29 = bf16[8,128,512]{1,2,0:T(8,128)(2,1)S(1)} all-to-all(bf16[8,128,512]{1,2,0:T(8,128)(2,1)S(1)} %broadcast_select_fusion), channel_id=1, replica_groups=mesh['vocab'=4,'expert'=8] {'expert'}, dimensions={0} | all-to-all | bytes 2097152 | tf_op jit(solution)/shard_map/all_to_all | solution.py:70
  48.8 1.3 copy.34
  50.1 0.0 reduce-scatter.10.cloned.1.call-update
  50.1 0.0 all-gather.2.cloned.1.call-start
  50.2 0.0 copy-done.2
  50.2 19.2 %all_to_all.30 = bf16[4,32,1024]{2,1,0:T(8,128)(2,1)S(1)} all-to-all(bf16[4,32,1024]{2,1,0:T(8,128)(2,1)S(1)} %bitcast.33), channel_id=1, replica_groups=mesh['vocab'=4,'expert'=8] {'vocab'}, dimensions={0} | all-to-all | bytes 524288 | tf_op jit(solution)/shard_map/all_to_all | solution.py:62
  69.5 10.3 %reduce-scatter.10.cloned.1.call-done = bf16[32,4096]{1,0:T(8,128)(2,1)} async-done(((bf16[128,4096]{1,0:T(8,128)(2,1)}), bf16[32,4096]{1,0:T(8,128)(2,1)}) %reduce-scatter.10.cloned.1.call-update) | async-done | bytes 262160 | tf_op jit(solution)/shard_map/reduce_scatter | solution.py:71
  79.8 1.2 fusion.11
  80.9 0.0 copy-done.3
  81.0 1.8 fusion.9
  82.7 0.0 all-gather.2.cloned.1.call-update
  82.8 0.0 reduce-scatter.6.cloned.1.call-start
  82.8 0.0 copy-done.5
  82.9 0.0 copy-done.6
  82.9 9.1 %all_gather.7 = f32[1024,16]{0,1:T(8,128)S(1)} all-gather(f32[128,16]{0,1:T(8,128)S(1)} %select_reduce_fusion), channel_id=1, replica_groups=mesh['vocab'=4,'expert'=8] {'expert'}, dimensions={0}, use_global_device_ids=true | all-gather | bytes 73728 | tf_op jit(solution)/shard_map/all_gather | solution.py:60
  92.0 67.3 %all-gather.2.cloned.1.call-done = bf16[1024,4096]{1,0:T(8,128)(2,1)} async-done(((bf16[32,4096]{1,0:T(8,128)(2,1)}), bf16[1024,4096]{1,0:T(8,128)(2,1)}) %all-gather.2.cloned.1.call-update) | async-done | bytes 8388624 | tf_op jit(solution)/shard_map/all_gather | solution.py:75
  159.3 0.0 copy-start.8
  159.3 0.0 slice-start
  159.3 11.0 %fusion.1 = f32[1024,768]{1,0:T(8,128)S(1)} fusion(bf16[1024,4096]{1,0:T(8,128)(2,1)} %all-gather.2.cloned.1.call-done, bf16[1,4096,768]{2,1,0:T(8,128)(2,1)} %param.24), kind=kOutput, calls=%fused_computation.4 | convolution fusion | flops 6442450944 | bytes 17825792 | tf_op jit(solution)/shard_map/dot_general | solution.py:81
  170.4 0.0 copy-done.8
  170.4 0.0 slice-start.1
  170.4 9.9 %multiply_convert_fusion.1 = bf16[1024,768]{1,0:T(8,128)(2,1)S(1)} fusion(f32[1024,768]{1,0:T(8,128)S(1)} %fusion.1, bf16[1024,4096]{1,0:T(8,128)(2,1)S(1)} %copy-done.8, bf16[1,4096,768]{2,1,0:T(8,128)(2,1)} %param.23), kind=kOutput, calls=%fused_computation.8 | convolution fusion | flops 6447169536 | bytes 19398656 | tf_op jit(solution)/shard_map/dot_general | solution.py:80
  180.3 0.0 slice-done
  180.3 0.0 slice-done.1
  180.4 8.9 %multiply_convert_fusion = bf16[1024,4096]{1,0:T(8,128)(2,1)} fusion(f32[1024]{0:T(1024)S(1)} %bitcast.34, bf16[1024,768]{1,0:T(8,128)(2,1)S(1)} %multiply_convert_fusion.1, bf16[1,768,4096]{2,1,0:T(8,128)(2,1)S(1)} %bitcast.36), kind=kOutput, calls=%fused_computation.2 | convolution fusion | flops 6450839552 | bytes 16257024 | tf_op jit(solution)/shard_map/dot_general | solution.py:83
  189.2 0.0 copy-start.1
  189.2 0.0 copy-start.4
  189.2 0.0 copy-start.7
  189.2 0.0 reduce-scatter.6.cloned.1.call-update
  189.3 0.0 reduce-scatter.8.cloned.1.call-start
  189.3 0.1 broadcast_in_dim.55
  189.4 0.8 copy-done.1
  190.2 0.0 copy-done.4
  190.2 0.1 constant_dynamic-update-slice_fusion.3
  190.3 1.6 collective-permute-start
  191.9 67.4 %reduce-scatter.6.cloned.1.call-done = bf16[128,4096]{1,0:T(8,128)(2,1)} async-done(((bf16[1024,4096]{1,0:T(8,128)(2,1)}), bf16[128,4096]{1,0:T(8,128)(2,1)}) %reduce-scatter.6.cloned.1.call-update) | async-done | bytes 1048592 | tf_op jit(solution)/shard_map/reduce_scatter | solution.py:85
  259.3 0.0 reduce-scatter.8.cloned.1.call-update
  259.4 3.4 %collective-permute-start.1 = (bf16[32,4096]{1,0:T(8,128)(2,1)S(1)}, bf16[32,4096]{1,0:T(8,128)(2,1)S(1)}, u32[]{:S(2)}, u32[]{:S(2)}) collective-permute-start(bf16[32,4096]{1,0:T(8,128)(2,1)S(1)} %get-tuple-element.13), channel_id=1, source_target_pairs={{0,24},{8,0},{16,8},{24,16},{1,25},{9,1},{17,9},{25,17},{2,26},{10... | collective-permute-start | bytes 786440 | tf_op jit(solution)/shard_map/ppermute | solution.py:21
  262.8 0.0 collective-permute-done
  262.8 0.0 collective-permute-start.2
  262.8 8.2 %collective-permute-done.1 = bf16[32,4096]{1,0:T(8,128)(2,1)S(1)} collective-permute-done((bf16[32,4096]{1,0:T(8,128)(2,1)S(1)}, bf16[32,4096]{1,0:T(8,128)(2,1)S(1)}, u32[]{:S(2)}, u32[]{:S(2)}) %collective-permute-start.1) | collective-permute-done | bytes 262176 | tf_op jit(solution)/shard_map/ppermute | solution.py:21
  271.0 10.1 %collective-permute-done.2 = bf16[32,4096]{1,0:T(8,128)(2,1)S(1)} collective-permute-done((bf16[32,4096]{1,0:T(8,128)(2,1)S(1)}, bf16[32,4096]{1,0:T(8,128)(2,1)S(1)}, u32[]{:S(2)}, u32[]{:S(2)}) %collective-permute-start.2) | collective-permute-done | bytes 262176 | tf_op jit(solution)/shard_map/ppermute | solution.py:16
  281.1 0.0 copy-done
  281.1 0.6 multiply_reduce_fusion
  281.7 0.0 copy-done.7
  281.7 0.1 multiply_convert_fusion.2
  281.8 0.7 copy.33
  282.5 10.1 %reduce-scatter.8.cloned.1.call-done = bf16[128,1024]{1,0:T(8,128)(2,1)} async-done(((bf16[128,4096]{1,0:T(8,128)(2,1)}), bf16[128,1024]{1,0:T(8,128)(2,1)}) %reduce-scatter.8.cloned.1.call-update) | async-done | bytes 262160 | tf_op jit(solution)/shard_map/reduce_scatter | solution.py:86
  (14 shorter events, 0.2 us)
Async XLA Ops:
  7.2 274.0 %copy-start = (bf16[4096,128]{1,0:T(8,128)(2,1)S(1)}, bf16[4096,128]{1,0:T(8,128)(2,1)}, u32[]{:S(2)}) copy-start(bf16[4096,128]{1,0:T(8,128)(2,1)} %param.18) | copy-start | bytes 3145732
  7.2 72.6 %reduce-scatter.10.cloned.1.call-start = ((), (), s32[]{:S(2)}) async-start(), calls=%async_computation.8 | async-start | bytes 1310720 | tf_op jit(solution)/shard_map/reduce_scatter | solution.py:71
  27.7 22.5 %copy-start.2 = (bf16[128,1024]{1,0:T(8,128)(2,1)S(1)}, bf16[128,1024]{1,0:T(8,128)(2,1)}, u32[]{:S(2)}) copy-start(bf16[128,1024]{1,0:T(8,128)(2,1)} %param.16) | copy-start | bytes 786436
  27.7 53.3 %copy-start.3 = (f32[4096]{0:T(1024)S(1)}, f32[4096]{0:T(1024)}, u32[]{:S(2)}) copy-start(f32[4096]{0:T(1024)} %param.20) | copy-start | bytes 49156
  28.3 54.5 %copy-start.5 = (s32[128,8]{0,1:T(8,128)S(1)}, s32[128,8]{0,1:T(8,128)}, u32[]{:S(2)}) copy-start(s32[128,8]{0,1:T(8,128)} %param.22) | copy-start | bytes 12292
  28.4 54.5 %copy-start.6 = (s32[128,8]{0,1:T(8,128)S(1)}, s32[128,8]{0,1:T(8,128)}, u32[]{:S(2)}) copy-start(s32[128,8]{0,1:T(8,128)} %param.21) | copy-start | bytes 12292
  50.1 109.2 %all-gather.2.cloned.1.call-start = ((), (), s32[]{:S(2)}) async-start(), calls=%async_computation.5 | async-start | bytes 8650752 | tf_op jit(solution)/shard_map/all_gather | solution.py:75
  82.8 176.5 %reduce-scatter.6.cloned.1.call-start = ((), (), s32[]{:S(2)}) async-start(), calls=%async_computation.6 | async-start | bytes 9437184 | tf_op jit(solution)/shard_map/reduce_scatter | solution.py:85
  159.3 11.1 %copy-start.8 = (bf16[1024,4096]{1,0:T(8,128)(2,1)S(1)}, bf16[1024,4096]{1,0:T(8,128)(2,1)}, u32[]{:S(2)}) copy-start(bf16[1024,4096]{1,0:T(8,128)(2,1)} %all-gather.2.cloned.1.call-done) | copy-start | bytes 25165828
  159.3 21.0 %slice-start = ((s8[6291456]{0:T(1024)(128)(4,1)}), s8[4194304]{0:T(1024)(128)(4,1)S(1)}, s32[]{:S(2)}) async-start(s8[6291456]{0:T(1024)(128)(4,1)} %bitcast.35), calls=%async_computation.9 | async-start | bytes 8388608
  170.4 10.0 %slice-start.1 = ((s8[6291456]{0:T(1024)(128)(4,1)}), s8[2097152]{0:T(1024)(128)(4,1)S(1)}, s32[]{:S(2)}) async-start(s8[6291456]{0:T(1024)(128)(4,1)} %bitcast.35), calls=%async_computation.10 | async-start | bytes 4194304
  189.2 0.9 copy-start.1
  189.2 1.0 copy-start.4
  189.2 92.5 %copy-start.7 = (f32[128]{0:T(128)S(1)}, f32[128]{0:T(128)}, u32[]{:S(2)}) copy-start(f32[128]{0:T(128)} %param.19) | copy-start | bytes 1540
  189.3 103.4 %reduce-scatter.8.cloned.1.call-start = ((), (), s32[]{:S(2)}) async-start(), calls=%async_computation.7 | async-start | bytes 1310720 | tf_op jit(solution)/shard_map/reduce_scatter | solution.py:86
  190.3 72.4 %collective-permute-start = (bf16[32,4096]{1,0:T(8,128)(2,1)S(1)}, bf16[32,4096]{1,0:T(8,128)(2,1)S(1)}, u32[]{:S(2)}, u32[]{:S(2)}) collective-permute-start(bf16[32,4096]{1,0:T(8,128)(2,1)S(1)} %get-tuple-element.13), channel_id=1, source_target_pairs={{0,8},{8,16},{16,24},{24,0},{1,9},{9,17},{17,25},{25,1},{2,10},{10... | collective-permute-start | bytes 786440 | tf_op jit(solution)/shard_map/ppermute | solution.py:16
  259.4 11.6 %collective-permute-start.1 = (bf16[32,4096]{1,0:T(8,128)(2,1)S(1)}, bf16[32,4096]{1,0:T(8,128)(2,1)S(1)}, u32[]{:S(2)}, u32[]{:S(2)}) collective-permute-start(bf16[32,4096]{1,0:T(8,128)(2,1)S(1)} %get-tuple-element.13), channel_id=1, source_target_pairs={{0,24},{8,0},{16,8},{24,16},{1,25},{9,1},{17,9},{25,17},{2,26},{10... | collective-permute-start | bytes 786440 | tf_op jit(solution)/shard_map/ppermute | solution.py:21
  262.8 18.4 %collective-permute-start.2 = (bf16[32,4096]{1,0:T(8,128)(2,1)S(1)}, bf16[32,4096]{1,0:T(8,128)(2,1)S(1)}, u32[]{:S(2)}, u32[]{:S(2)}) collective-permute-start(bf16[32,4096]{1,0:T(8,128)(2,1)S(1)} %collective-permute-done), channel_id=1, source_target_pairs={{0,8},{8,16},{16,24},{24,0},{1,9},{9,17},{17,25},{25,1},{2,10},{10... | collective-permute-start | bytes 786440 | tf_op jit(solution)/shard_map/ppermute | solution.py:16
Sparse Core Ops, SparseCore 0:
  50.2 29.4 reduce-scatter.9
  83.7 75.5 all-gather.1
  189.4 69.8 reduce-scatter.5
  262.0 30.6 reduce-scatter.7
